TPU v7x, 32 devices: a whole 2x2x4 slice. The times are simulated.
32 devices in a mesh: sec: 2 (over core), grp: 4 (over y, x), dev: 4 (over z).
Axes of the slice: x: 2, y: 2, z: 4, core: 2. Of those that a mesh axis runs over, the one named last changes fastest.
Arguments:
- current: float32 [32, 196608], P(None, ('sec', 'grp', 'dev')), may hold values from -6 to 6
- prior: float32 [8, 32, 196608], P(None, None, ('sec', 'grp', 'dev')), as said below
- block_values: float32 [1024, 6, 9216], P(('grp', 'dev')), may hold values from -0.25 to 0.25
- block_cols: int32 [1024, 6], P(('grp', 'dev')), may hold values from 0 to 63
- face_match: int32 [16, 4, 1536], P(('grp', 'dev')), may hold values from 0 to 1535, each once within a row
- face_weight: float32 [16, 4, 1536], P(('grp', 'dev')), may hold values from -3 to 3
- fluid_diag: float32 [98304], P(('grp', 'dev')), may hold values from 2 to 4
- wet_source: int32 [49152], P(('grp', 'dev')), may hold values from 0 to 6143
- wet_dest: int32 [49152, 1], P(('grp', 'dev')), may hold values from 0 to 15; in each aligned block of 3072 rows (0 to 3071, 3072 to 6143, ...) at most 392 rows name the same one
- wet_target: int32 [49152], P(('grp', 'dev')), may hold values from 0 to 6143
- wet_weight: float32 [49152], P(('grp', 'dev')), may hold values from -5 to 5
Outputs:
- next_block: float32 [32, 196608], P(None, ('sec', 'grp', 'dev'))
- coeffs: float32 [8, 32, 32], replicated
- rfac: float32 [32, 32], replicated
Inputs may be any that keep to these rules, and one draw needn't show every extreme that they name: `block_cols`: block columns index blocks within the same subdomain. `face_match`: each subdomain's matching of one round is a permutation of its face. `prior`: each earlier block's columns have about unit length. `wet_dest`: among one structure subdomain's couplings, at most 392 name the same fluid subdomain, and some subdomain has exactly 392 for one.
All inputs are finite; a program needn't handle non-finite values.
Results may differ from a plain program's by a relative error of at most 0.00008.
Values sent between devices are 32-bit elements; how exact they have to be, the bound alone decides.
A program may use at most 128 MiB of HBM per device.

v0:
```python
import jax
import jax.numpy as jnp
from jax import lax
from jax.sharding import PartitionSpec as P

BS = 96
NB = 6
ROUNDS = 4


def swapped(block, axis, bit):
    count = lax.axis_size(axis)
    route = []
    for low in range(count):
        high = low | 1 << bit
        if high != low and high < count:
            route += [(low, high), (high, low)]
    return lax.ppermute(block, axis, route)


def with_halo(x, sides, width):
    for axis, dim in sides:
        count, length = (lax.axis_size(axis), x.shape[dim])
        up = [(i, (i + 1) % count) for i in range(count - 1)]
        down = [(j, i) for i, j in up]
        last = lax.slice_in_dim(x, length - width, length, axis=dim)
        initial = lax.slice_in_dim(x, 0, width, axis=dim)
        before = lax.ppermute(last, axis, up)
        after = lax.ppermute(initial, axis, down)
        x = jnp.concatenate([before, x, after], axis=dim)
    return x


def shards(
    current,
    prior,
    block_values,
    block_cols,
    face_match,
    face_weight,
    fluid_diag,
    wet_source,
    wet_dest,
    wet_target,
    wet_weight,
):
    highest = lax.Precision.HIGHEST
    width = current.shape[0]
    local_rows = current.shape[1]
    face_rows = face_match.shape[2]
    row_blocks = block_cols.shape[0]
    wet_slots = wet_source.shape[0]
    subdomains = lax.axis_size("grp") * lax.axis_size("dev")
    total_rows = local_rows * lax.axis_size("sec") * subdomains
    capacity = 2 * wet_slots // subdomains + 8
    is_shell = lax.axis_index("sec") == 0
    senders = jnp.where(is_shell, 1.0, 0.0).astype(jnp.float32)
    partner_faces = []
    for sweep in range(ROUNDS):
        face_now = current[:, sweep * face_rows : (sweep + 1) * face_rows]
        if sweep < 2:
            partner_faces.append(swapped(face_now, "dev", sweep))
        else:
            partner_faces.append(swapped(face_now, "grp", sweep - 2))
    padded = with_halo(current, ((("grp", "dev"), 1),), 1)
    destination = wet_dest[:, 0]
    onehot = (destination[:, None] == jnp.arange(subdomains, dtype=jnp.int32)[None, :]).astype(
        jnp.int32
    )
    ranks = jnp.cumsum(onehot, axis=0) - 1
    slot = jnp.sum(ranks * onehot, axis=1)
    moved = (wet_weight * senders)[None, :] * current[:, wet_source]
    target_float = wet_target.astype(jnp.float32) * senders
    buffer = jnp.zeros((2 * subdomains, width, capacity), jnp.float32)
    buffer = buffer.at[destination + subdomains, :, slot].set(moved.T)
    row_buffer = jnp.zeros((2 * subdomains, capacity), jnp.float32)
    row_buffer = row_buffer.at[destination + subdomains, slot].set(target_float)
    got_values, got_rows = (
        lax.all_to_all(buffer, ("sec", "grp", "dev"), split_axis=0, concat_axis=0, tiled=True),
        lax.all_to_all(row_buffer, ("sec", "grp", "dev"), split_axis=0, concat_axis=0, tiled=True),
    )
    incoming = jnp.moveaxis(got_values, 1, 0).reshape(width, -1)
    incoming_rows = got_rows.reshape(-1).astype(jnp.int32)

    def shell_apply(vector):
        picked = vector.reshape(width, row_blocks, BS)[:, block_cols, :]
        matrices = block_values.reshape(row_blocks, NB, BS, BS)
        result = jnp.einsum("kibc,ibrc->kir", picked, matrices, precision=highest).reshape(
            width, local_rows
        )
        for sweep in range(ROUNDS):
            matched = partner_faces[sweep][:, face_match[0, sweep]]
            result = result.at[:, sweep * face_rows : (sweep + 1) * face_rows].add(
                face_weight[0, sweep][None, :] * matched
            )
        return result

    def fluid_apply(vector):
        before = padded[:, :-2]
        after = padded[:, 2:]
        result = fluid_diag[None, :] * vector - before - after
        return result.at[:, incoming_rows].add(incoming)

    image = lax.cond(is_shell, shell_apply, fluid_apply, current)
    h_first = lax.psum(
        jnp.einsum("jkr,lr->jkl", prior, image, precision=highest), ("sec", "grp", "dev")
    )
    w_one = image - jnp.einsum("jkl,jkr->lr", h_first, prior, precision=highest)
    h_second = lax.psum(
        jnp.einsum("jkr,lr->jkl", prior, w_one, precision=highest), ("sec", "grp", "dev")
    )
    w_two = w_one - jnp.einsum("jkl,jkr->lr", h_second, prior, precision=highest)
    gram = lax.psum(jnp.dot(w_two, w_two.T, precision=highest), ("sec", "grp", "dev")) / total_rows
    coeffs = h_first + h_second
    factor = jnp.linalg.cholesky(gram)
    next_block = lax.linalg.triangular_solve(factor, w_two, left_side=True, lower=True)
    return (next_block, coeffs, factor.T)


def solution(mesh):
    placed = (
        P(None, ("sec", "grp", "dev")),
        P(None, None, ("sec", "grp", "dev")),
        P(("grp", "dev"), None, None),
        P(("grp", "dev"), None),
        P(("grp", "dev"), None, None),
        P(("grp", "dev"), None, None),
        P(("grp", "dev")),
        P(("grp", "dev")),
        P(("grp", "dev"), None),
        P(("grp", "dev")),
        P(("grp", "dev")),
    )
    return jax.shard_map(
        shards,
        mesh=mesh,
        in_specs=placed,
        out_specs=(P(None, ("sec", "grp", "dev")), P(), P()),
        check_vma=False,
    )
```

profile of v0, /device:TPU:0, one launch (start us, length us, event | category | flops | bytes accessed | tf_op | source)
XLA Modules:
  0.0 426.9 jit_solution(6008046726579395630)
XLA Ops:
  1.4 4.6 %reduce-window.6 = s32[16,24,128]{2,1,0:T(8,128)S(1)} reduce-window(s32[16,24,128]{2,1,0:T(8,128)S(1)} %fusion.27, s32[]{:T(128)} %constant.179.clone.1), window={size=1x1x128 pad=0_0x0_0x127_0}, to_apply=%region_0.1 | reduce-window | flops 6242304 | bytes 393220 | tf_op jit(solution)/shard_map/reduce-window
  6.7 0.8 fusion.26
  8.2 0.8 and_reduce_fusion
  10.5 11.8 %scatter_custom_fusion.1 = f32[12544]{0:T(1024)S(1)} fusion(s32[3072]{0:T(1024)S(1)} %broadcast_select_fusion, f32[3072]{0:T(1024)S(1)} %get-tuple-element.233, f32[]{:T(128)} %constant.180.clone.1), kind=kCustom, calls=%fused_computation.71 | custom fusion | bytes 50180
  22.3 0.8 all_to_all.9
  23.1 7.3 %all-to-all-start = ((f32[32,1,392]{2,1,0:T(1,128)}), f32[32,1,392]{2,1,0:T(1,128)S(1)}, u32[]{:S(2)}, u32[]{:S(2)}) async-start(f32[32,1,392]{2,1,0:T(1,128)} %all_to_all.9), calls=%async_computation | async-start | bytes 131072 | tf_op jit(solution)/shard_map/all_to_all | solution.py:80
  31.2 2.0 copy.123
  33.1 20.8 %scatter_custom_fusion.2 = f32[12544,32]{1,0:T(8,128)} fusion(s32[3072]{0:T(1024)S(1)} %broadcast_select_fusion, f32[]{:T(128)} %constant.180.clone.1, f32[3072]{0:T(1024)S(1)} %get-tuple-element.234, f32[32,6144]{0,1:T(8,128)S(1)} %copy.123, s32[3072]{0:T(1024)S(1)} %fusion.34), kind=kCustom, calls=%fused_computation.50 | custom fusion | flops 98304 | bytes 4775940
  53.9 6.0 %copy.125 = f32[32,32,392]{2,1,0:T(8,128)} copy(f32[32,32,392]{1,2,0:T(8,128)} %bitcast.92) | data formatting | bytes 3211264 | tf_op jit(solution)/shard_map/scatter | solution.py:75
  60.0 5.8 %all-to-all-start.1 = ((f32[32,32,392]{2,1,0:T(8,128)}), f32[32,32,392]{2,1,0:T(8,128)S(1)}, u32[]{:S(2)}, u32[]{:S(2)}) async-start(f32[32,32,392]{2,1,0:T(8,128)} %copy.125), calls=%async_computation.1 | async-start | bytes 4194304 | tf_op jit(solution)/shard_map/all_to_all | solution.py:79
  65.9 0.8 fusion.36
  66.7 1.8 collective-permute-start.2
  68.4 2.4 collective-permute-start.3
  70.8 1.5 collective-permute-start.4
  72.3 1.5 collective-permute-start.5
  73.9 2.4 collective-permute-start
  76.3 33.0 %collective-permute-done = f32[32,1]{1,0:T(8,128)S(1)} collective-permute-done((f32[32,1]{1,0:T(8,128)S(1)}, f32[32,1]{1,0:T(8,128)S(1)}, u32[]{:S(2)}, u32[]{:S(2)}) %collective-permute-start) | collective-permute-done | bytes 160 | tf_op jit(solution)/shard_map/ppermute | solution.py:28
  109.3 1.3 collective-permute-start.1
  110.6 15.2 %collective-permute-done.1 = f32[32,1]{1,0:T(8,128)S(1)} collective-permute-done((f32[32,1]{1,0:T(8,128)S(1)}, f32[32,1]{1,0:T(8,128)S(1)}, u32[]{:S(2)}, u32[]{:S(2)}) %collective-permute-start.1) | collective-permute-done | bytes 160 | tf_op jit(solution)/shard_map/ppermute | solution.py:29
  125.8 1.2 concatenate.15
  127.1 81.7 %conditional.1 = (f32[32,6144]{0,1:T(8,128)}) conditional(s32[]{:T(128)} %convert_element_type.23, (f32[6144]{0:T(1024)S(1)}, f32[32,6144]{1,0:T(8,128)S(1)}, f32[32,6146]{1,0:T(8,128)}, f32[32,1,392]{2,1,0:T(1,128)S(1)}, f32[32,32,392]{2,0,1:T(8,128)S(1)}) %tuple.73, (f32[32,6144]{1,0:T(8,128)S(1)}, s32[64,6]{0,1:T(8,128)S(1)}, ...), branch_computations={%region_5.7_spmd, %region_7.11_spmd} | conditional | flops 1359523968 | bytes 72574472 | solution.py:104
  135.6 3.8 gather_fusion
  139.4 17.6 %reshape.288 = f32[64,6,96,96]{3,2,0,1:T(8,128)} reshape(f32[64,6,9216]{2,0,1:T(8,128)} %get-tuple-element.106) | data formatting | bytes 28311552 | tf_op jit(solution)/shard_map/cond/branch_1_fun/reshape | solution.py:87
  157.0 20.7 %fusion.2 = f32[32,64,96]{2,0,1:T(8,128)S(1)} fusion(f32[32,64,6,96]{3,0,2,1:T(8,128)} %bitcast.91, f32[64,6,96,96]{3,2,0,1:T(8,128)} %reshape.288), kind=kOutput, calls=%fused_computation.11 | convolution fusion | flops 1358954496 | bytes 19660800 | tf_op jit(solution)/shard_map/cond/branch_1_fun/kibc,ibrc->kir/dot_general | solution.py:88
  177.7 2.3 copy.146
  180.0 1.2 copy.130
  181.3 2.6 gather_fusion.1
  184.6 2.9 fusion.5
  187.6 1.2 copy.131
  188.8 2.6 gather_fusion.2
  192.0 2.9 fusion.6
  194.9 1.2 copy.132
  196.1 2.6 gather_fusion.3
  199.4 3.0 fusion.7
  202.4 1.2 copy.133
  203.6 2.6 gather_fusion.4
  206.2 2.4 fusion.8
  208.7 2.3 copy.135
  211.1 22.2 %fusion.20 = f32[8,32,32]{1,2,0:T(8,128)S(1)} fusion(f32[8,32,6144]{2,1,0:T(8,128)} %param.22, f32[32,6144]{0,1:T(8,128)} %get-tuple-element.235), kind=kOutput, calls=%fused_computation.56 | convolution fusion | flops 603979776 | bytes 7110656 | tf_op jit(solution)/shard_map/jkr,lr->jkl/dot_general | solution.py:106
  233.2 70.2 %psum.21 = f32[8,32,32]{1,2,0:T(8,128)S(1)} all-reduce(f32[8,32,32]{1,2,0:T(8,128)S(1)} %fusion.20), channel_id=1, replica_groups=mesh['sec'=2,'grp'=4,'dev'=4] {'sec','grp','dev'}, use_global_device_ids=true, to_apply=%region_11.12 | all-reduce | flops 8192 | bytes 65536 | tf_op jit(solution)/shard_map/psum | solution.py:105
  303.4 7.5 %convolution_bitcast_fusion.1 = f32[32,6144]{1,0:T(8,128)S(1)} fusion(f32[8,32,32]{1,2,0:T(8,128)S(1)} %psum.21, f32[8,32,6144]{2,1,0:T(8,128)} %param.22), kind=kOutput, calls=%fused_computation.48 | convolution fusion | flops 603979776 | bytes 7110656 | tf_op jit(solution)/shard_map/jkl,jkr->lr/dot_general | solution.py:108
  311.1 16.3 %convolution_bitcast_fusion.2 = f32[8,32,32]{1,2,0:T(8,128)S(1)} fusion(f32[8,32,6144]{2,1,0:T(8,128)} %param.22, f32[32,6144]{1,0:T(8,128)S(1)} %sub.23), kind=kOutput, calls=%fused_computation.55 | convolution fusion | flops 603979776 | bytes 7110656 | tf_op jit(solution)/shard_map/jkr,lr->jkl/dot_general | solution.py:110
  327.4 41.1 %psum.22 = f32[8,32,32]{1,2,0:T(8,128)S(1)} all-reduce(f32[8,32,32]{1,2,0:T(8,128)S(1)} %convolution_bitcast_fusion.2), channel_id=1, replica_groups=mesh['sec'=2,'grp'=4,'dev'=4] {'sec','grp','dev'}, use_global_device_ids=true, to_apply=%region_12.13 | all-reduce | flops 8192 | bytes 65536 | tf_op jit(solution)/shard_map/psum | solution.py:109
  368.5 7.6 %fusion.14 = f32[32,6144]{1,0:T(8,128)S(1)} fusion(f32[32,6144]{1,0:T(8,128)S(1)} %sub.23, f32[8,32,32]{1,2,0:T(8,128)S(1)} %psum.22, f32[8,32,6144]{2,1,0:T(8,128)} %param.22), kind=kOutput, calls=%fused_computation.49 | convolution fusion | flops 604176384 | bytes 7897088 | tf_op jit(solution)/shard_map/jkl,jkr->lr/dot_general | solution.py:112
  376.8 39.9 %psum.23 = f32[32,32]{0,1:T(8,128)S(1)} all-reduce(f32[32,32]{0,1:T(8,128)S(1)} %fusion.38), channel_id=1, replica_groups=mesh['sec'=2,'grp'=4,'dev'=4] {'sec','grp','dev'}, use_global_device_ids=true, to_apply=%region_13.14 | all-reduce | flops 1024 | bytes 8192 | tf_op jit(solution)/shard_map/psum | solution.py:113
  416.8 2.9 cholesky.16
  421.1 2.4 custom-call.6
  423.5 1.7 fusion.30
  (50 shorter events, 11.6 us)
Async XLA Ops:
  23.1 36.9 %all-to-all-start = ((f32[32,1,392]{2,1,0:T(1,128)}), f32[32,1,392]{2,1,0:T(1,128)S(1)}, u32[]{:S(2)}, u32[]{:S(2)}) async-start(f32[32,1,392]{2,1,0:T(1,128)} %all_to_all.9), calls=%async_computation | async-start | bytes 131072 | tf_op jit(solution)/shard_map/all_to_all | solution.py:80
  60.0 5.9 %copy-start = (f32[32,6144]{1,0:T(8,128)S(1)}, f32[32,6144]{1,0:T(8,128)}, u32[]{:S(2)}) copy-start(f32[32,6144]{1,0:T(8,128)} %param.21) | copy-start | bytes 2359300
  60.0 67.0 %copy-start.3 = (f32[1,4,1536]{2,1,0:T(4,128)S(1)}, f32[1,4,1536]{2,1,0:T(4,128)}, u32[]{:S(2)}) copy-start(f32[1,4,1536]{2,1,0:T(4,128)} %param.26) | copy-start | bytes 73732
  60.0 67.0 %copy-start.4 = (s32[1,4,1536]{2,1,0:T(4,128)S(1)}, s32[1,4,1536]{2,1,0:T(4,128)}, u32[]{:S(2)}) copy-start(s32[1,4,1536]{2,1,0:T(4,128)} %param.25) | copy-start | bytes 73732
  60.0 67.1 %copy-start.5 = (f32[6144]{0:T(1024)S(1)}, f32[6144]{0:T(1024)}, u32[]{:S(2)}) copy-start(f32[6144]{0:T(1024)} %param.27) | copy-start | bytes 73732
  60.0 67.1 %copy-start.6 = (s32[64,6]{0,1:T(8,128)S(1)}, s32[64,6]{0,1:T(8,128)}, u32[]{:S(2)}) copy-start(s32[64,6]{0,1:T(8,128)} %param.24) | copy-start | bytes 4612
  60.0 67.0 %all-to-all-start.1 = ((f32[32,32,392]{2,1,0:T(8,128)}), f32[32,32,392]{2,1,0:T(8,128)S(1)}, u32[]{:S(2)}, u32[]{:S(2)}) async-start(f32[32,32,392]{2,1,0:T(8,128)} %copy.125), calls=%async_computation.1 | async-start | bytes 4194304 | tf_op jit(solution)/shard_map/all_to_all | solution.py:79
  66.7 60.3 %collective-permute-start.2 = (f32[32,1536]{1,0:T(8,128)}, f32[32,1536]{1,0:T(8,128)}, u32[]{:S(2)}, u32[]{:S(2)}) collective-permute-start(f32[32,1536]{1,0:T(8,128)} %get-tuple-element.226), channel_id=1, source_target_pairs={{0,1},{1,0},{2,3},{3,2},{4,5},{5,4},{6,7},{7,6},{8,9},{9,8},{10,11... | collective-permute-start | bytes 589832 | tf_op jit(solution)/shard_map/ppermute | solution.py:18
  68.4 58.6 %collective-permute-start.3 = (f32[32,1536]{1,0:T(8,128)}, f32[32,1536]{1,0:T(8,128)}, u32[]{:S(2)}, u32[]{:S(2)}) collective-permute-start(f32[32,1536]{1,0:T(8,128)} %get-tuple-element.225), channel_id=1, source_target_pairs={{0,2},{2,0},{1,3},{3,1},{4,6},{6,4},{5,7},{7,5},{8,10},{10,8},{9,1... | collective-permute-start | bytes 589832 | tf_op jit(solution)/shard_map/ppermute | solution.py:18
  70.8 56.1 %collective-permute-start.4 = (f32[32,1536]{1,0:T(8,128)S(1)}, f32[32,1536]{1,0:T(8,128)}, u32[]{:S(2)}, u32[]{:S(2)}) collective-permute-start(f32[32,1536]{1,0:T(8,128)S(1)} %get-tuple-element.224), channel_id=1, source_target_pairs={{0,4},{4,0},{8,12},{12,8},{1,5},{5,1},{9,13},{13,9},{2,6},{6,2},{1... | collective-permute-start | bytes 589832 | tf_op jit(solution)/shard_map/ppermute | solution.py:18
  72.3 54.7 %collective-permute-start.5 = (f32[32,1536]{1,0:T(8,128)S(1)}, f32[32,1536]{1,0:T(8,128)}, u32[]{:S(2)}, u32[]{:S(2)}) collective-permute-start(f32[32,1536]{1,0:T(8,128)S(1)} %get-tuple-element.223), channel_id=1, source_target_pairs={{0,8},{8,0},{4,12},{12,4},{1,9},{9,1},{5,13},{13,5},{2,10},{10,2},... | collective-permute-start | bytes 589832 | tf_op jit(solution)/shard_map/ppermute | solution.py:18
  73.9 35.4 %collective-permute-start = (f32[32,1]{1,0:T(8,128)S(1)}, f32[32,1]{1,0:T(8,128)S(1)}, u32[]{:S(2)}, u32[]{:S(2)}) collective-permute-start(f32[32,1]{1,0:T(8,128)S(1)} %get-tuple-element.228), channel_id=1, source_target_pairs={{0,1},{1,2},{2,3},{3,4},{4,5},{5,6},{6,7},{7,8},{8,9},{9,10},{10,1... | collective-permute-start | bytes 392 | tf_op jit(solution)/shard_map/ppermute | solution.py:28
  109.3 16.5 %collective-permute-start.1 = (f32[32,1]{1,0:T(8,128)S(1)}, f32[32,1]{1,0:T(8,128)S(1)}, u32[]{:S(2)}, u32[]{:S(2)}) collective-permute-start(f32[32,1]{1,0:T(8,128)S(1)} %get-tuple-element.227), channel_id=1, source_target_pairs={{1,0},{2,1},{3,2},{4,3},{5,4},{6,5},{7,6},{8,7},{9,8},{10,9},{11,1... | collective-permute-start | bytes 392 | tf_op jit(solution)/shard_map/ppermute | solution.py:29
where the time goes:
time: 434 us; the launch traced here: 427 us
  blocking collectives  151 us (35%)
  matrix products  76.7 us (18%)
  local copies, waits for them, and re-layouts  67.1 us (15%)
  other arithmetic  51 us (12%)
  waiting for transfers between devices  48.2 us (11%)
  starting transfers between devices  24 us (6%)
  loops' own time  7.54 us (2%)
    psum x1, blocking collectives, shards(): lax.psum(jnp.einsum('jkr,lr->jkl', prior, image, precision=highest), ('se...  70.2 us
    psum x1, blocking collectives, shards(): lax.psum(jnp.einsum('jkr,lr->jkl', prior, w_one, precision=highest), ('se...  41.1 us
    psum x1, blocking collectives, shards(): lax.psum(jnp.dot(w_two, w_two.T, precision=highest), ('sec', 'grp', 'dev'))  39.9 us
    ppermute x1, waiting for transfers between devices, with_halo(): before = lax.ppermute(last, axis, up)  33 us
    unnamed x4, other arithmetic  22.4 us
    dot_general x1, matrix products, shards(): jnp.einsum('jkr,lr->jkl', prior, image, precision=highest)  22.2 us
    dot_general x1, matrix products, shell_apply(): jnp.einsum('kibc,ibrc->kir', picked, matrices, precision=highest)  20.7 us
    reshape x1, local copies, waits for them, and re-layouts, shell_apply(): matrices = block_values.reshape(row_blocks, NB, BS, BS)  17.6 us
  transfers between devices with their start and end apart: 8, of which 2 were waited for; matrix products, arithmetic and copies ran while one was open for 7% of the time, Pallas kernels for 0%

commit v1 on v0

--- a/solution.py
+++ b/solution.py
@@ -110,7 +110,10 @@
         jnp.einsum("jkr,lr->jkl", prior, w_one, precision=highest), ("sec", "grp", "dev")
     )
     w_two = w_one - jnp.einsum("jkl,jkr->lr", h_second, prior, precision=highest)
-    gram = lax.psum(jnp.dot(w_two, w_two.T, precision=highest), ("sec", "grp", "dev")) / total_rows
+    gram = (
+        lax.psum(lax.psum(jnp.dot(w_two, w_two.T, precision=highest), ("grp", "dev")), "sec")
+        / total_rows
+    )
     coeffs = h_first + h_second
     factor = jnp.linalg.cholesky(gram)
     next_block = lax.linalg.triangular_solve(factor, w_two, left_side=True, lower=True)

time: 434 us -> 473 us (1.090)
  blocking collectives: 151 us -> 190 us
    psum x1 -> x2, blocking collectives: 39.9 us -> 78.6 us  [the longest x1 75.2 us: shards(): lax.psum(jnp.dot(w_two, w_two.T, precision=highest), ('grp', 'dev'))]
where the time goes in v1:
time: 473 us; the launch traced here: 466 us
  blocking collectives  190 us (40%)
  matrix products  76.7 us (16%)
  local copies, waits for them, and re-layouts  67.1 us (14%)
  other arithmetic  51 us (11%)
  waiting for transfers between devices  48.2 us (10%)
  starting transfers between devices  24 us (5%)
  loops' own time  7.54 us (2%)
    psum x1, blocking collectives, shards(): lax.psum(jnp.dot(w_two, w_two.T, precision=highest), ('grp', 'dev'))  75.2 us
    psum x1, blocking collectives, shards(): lax.psum(jnp.einsum('jkr,lr->jkl', prior, image, precision=highest), ('se...  70.2 us
    psum x1, blocking collectives, shards(): lax.psum(jnp.einsum('jkr,lr->jkl', prior, w_one, precision=highest), ('se...  41.1 us
    ppermute x1, waiting for transfers between devices, with_halo(): before = lax.ppermute(last, axis, up)  33 us
    unnamed x4, other arithmetic  22.4 us
    dot_general x1, matrix products, shards(): jnp.einsum('jkr,lr->jkl', prior, image, precision=highest)  22.2 us
    dot_general x1, matrix products, shell_apply(): jnp.einsum('kibc,ibrc->kir', picked, matrices, precision=highest)  20.7 us
    reshape x1, local copies, waits for them, and re-layouts, shell_apply(): matrices = block_values.reshape(row_blocks, NB, BS, BS)  17.6 us
  transfers between devices with their start and end apart: 8, of which 2 were waited for; matrix products, arithmetic and copies ran while one was open for 7% of the time, Pallas kernels for 0%

profile of v1, /device:TPU:0, one launch (start us, length us, event | category | flops | bytes accessed | tf_op | source)
XLA Modules:
  0.0 465.6 jit_solution(11151272258576269114)
XLA Ops:
  1.4 4.6 reduce-window.6
  8.2 0.8 and_reduce_fusion
  10.5 11.8 %scatter_custom_fusion.1 = f32[12544]{0:T(1024)S(1)} fusion(s32[3072]{0:T(1024)S(1)} %broadcast_select_fusion, f32[3072]{0:T(1024)S(1)} %get-tuple-element.233, f32[]{:T(128)} %constant.180.clone.1), kind=kCustom, calls=%fused_computation.71 | custom fusion | bytes 50180
  22.3 0.8 all_to_all.9
  23.1 7.3 %all-to-all-start = ((f32[32,1,392]{2,1,0:T(1,128)}), f32[32,1,392]{2,1,0:T(1,128)S(1)}, u32[]{:S(2)}, u32[]{:S(2)}) async-start(f32[32,1,392]{2,1,0:T(1,128)} %all_to_all.9), calls=%async_computation | async-start | bytes 131072 | tf_op jit(solution)/shard_map/all_to_all | solution.py:80
  31.2 2.0 copy.123
  33.1 20.8 %scatter_custom_fusion.2 = f32[12544,32]{1,0:T(8,128)} fusion(s32[3072]{0:T(1024)S(1)} %broadcast_select_fusion, f32[]{:T(128)} %constant.180.clone.1, f32[3072]{0:T(1024)S(1)} %get-tuple-element.234, f32[32,6144]{0,1:T(8,128)S(1)} %copy.123, s32[3072]{0:T(1024)S(1)} %fusion.34), kind=kCustom, calls=%fused_computation.50 | custom fusion | flops 98304 | bytes 4775940
  53.9 6.0 %copy.125 = f32[32,32,392]{2,1,0:T(8,128)} copy(f32[32,32,392]{1,2,0:T(8,128)} %bitcast.92) | data formatting | bytes 3211264 | tf_op jit(solution)/shard_map/scatter | solution.py:75
  60.0 5.8 %all-to-all-start.1 = ((f32[32,32,392]{2,1,0:T(8,128)}), f32[32,32,392]{2,1,0:T(8,128)S(1)}, u32[]{:S(2)}, u32[]{:S(2)}) async-start(f32[32,32,392]{2,1,0:T(8,128)} %copy.125), calls=%async_computation.1 | async-start | bytes 4194304 | tf_op jit(solution)/shard_map/all_to_all | solution.py:79
  65.9 0.8 fusion.36
  66.7 1.8 collective-permute-start.2
  68.4 2.4 collective-permute-start.3
  70.8 1.5 collective-permute-start.4
  72.3 1.5 collective-permute-start.5
  73.9 2.4 collective-permute-start
  76.3 33.0 %collective-permute-done = f32[32,1]{1,0:T(8,128)S(1)} collective-permute-done((f32[32,1]{1,0:T(8,128)S(1)}, f32[32,1]{1,0:T(8,128)S(1)}, u32[]{:S(2)}, u32[]{:S(2)}) %collective-permute-start) | collective-permute-done | bytes 160 | tf_op jit(solution)/shard_map/ppermute | solution.py:28
  109.3 1.3 collective-permute-start.1
  110.6 15.2 %collective-permute-done.1 = f32[32,1]{1,0:T(8,128)S(1)} collective-permute-done((f32[32,1]{1,0:T(8,128)S(1)}, f32[32,1]{1,0:T(8,128)S(1)}, u32[]{:S(2)}, u32[]{:S(2)}) %collective-permute-start.1) | collective-permute-done | bytes 160 | tf_op jit(solution)/shard_map/ppermute | solution.py:29
  125.8 1.2 concatenate.15
  127.1 81.7 %conditional.1 = (f32[32,6144]{0,1:T(8,128)}) conditional(s32[]{:T(128)} %convert_element_type.23, (f32[6144]{0:T(1024)S(1)}, f32[32,6144]{1,0:T(8,128)S(1)}, f32[32,6146]{1,0:T(8,128)}, f32[32,1,392]{2,1,0:T(1,128)S(1)}, f32[32,32,392]{2,0,1:T(8,128)S(1)}) %tuple.73, (f32[32,6144]{1,0:T(8,128)S(1)}, s32[64,6]{0,1:T(8,128)S(1)}, ...), branch_computations={%region_5.7_spmd, %region_7.11_spmd} | conditional | flops 1359523968 | bytes 72574472 | solution.py:104
  135.6 3.8 gather_fusion
  139.4 17.6 %reshape.288 = f32[64,6,96,96]{3,2,0,1:T(8,128)} reshape(f32[64,6,9216]{2,0,1:T(8,128)} %get-tuple-element.106) | data formatting | bytes 28311552 | tf_op jit(solution)/shard_map/cond/branch_1_fun/reshape | solution.py:87
  157.0 20.7 %fusion.2 = f32[32,64,96]{2,0,1:T(8,128)S(1)} fusion(f32[32,64,6,96]{3,0,2,1:T(8,128)} %bitcast.91, f32[64,6,96,96]{3,2,0,1:T(8,128)} %reshape.288), kind=kOutput, calls=%fused_computation.11 | convolution fusion | flops 1358954496 | bytes 19660800 | tf_op jit(solution)/shard_map/cond/branch_1_fun/kibc,ibrc->kir/dot_general | solution.py:88
  177.7 2.3 copy.146
  180.0 1.2 copy.130
  181.3 2.6 gather_fusion.1
  184.6 2.9 fusion.5
  187.6 1.2 copy.131
  188.8 2.6 gather_fusion.2
  192.0 2.9 fusion.6
  194.9 1.2 copy.132
  196.1 2.6 gather_fusion.3
  199.4 3.0 fusion.7
  202.4 1.2 copy.133
  203.6 2.6 gather_fusion.4
  206.2 2.4 fusion.8
  208.7 2.3 copy.135
  211.1 22.2 %fusion.20 = f32[8,32,32]{1,2,0:T(8,128)S(1)} fusion(f32[8,32,6144]{2,1,0:T(8,128)} %param.22, f32[32,6144]{0,1:T(8,128)} %get-tuple-element.235), kind=kOutput, calls=%fused_computation.56 | convolution fusion | flops 603979776 | bytes 7110656 | tf_op jit(solution)/shard_map/jkr,lr->jkl/dot_general | solution.py:106
  233.2 70.2 %psum.28 = f32[8,32,32]{1,2,0:T(8,128)S(1)} all-reduce(f32[8,32,32]{1,2,0:T(8,128)S(1)} %fusion.20), channel_id=1, replica_groups=mesh['sec'=2,'grp'=4,'dev'=4] {'sec','grp','dev'}, use_global_device_ids=true, to_apply=%region_11.12 | all-reduce | flops 8192 | bytes 65536 | tf_op jit(solution)/shard_map/psum | solution.py:105
  303.4 7.5 %convolution_bitcast_fusion.1 = f32[32,6144]{1,0:T(8,128)S(1)} fusion(f32[8,32,32]{1,2,0:T(8,128)S(1)} %psum.28, f32[8,32,6144]{2,1,0:T(8,128)} %param.22), kind=kOutput, calls=%fused_computation.48 | convolution fusion | flops 603979776 | bytes 7110656 | tf_op jit(solution)/shard_map/jkl,jkr->lr/dot_general | solution.py:108
  311.1 16.3 %convolution_bitcast_fusion.2 = f32[8,32,32]{1,2,0:T(8,128)S(1)} fusion(f32[8,32,6144]{2,1,0:T(8,128)} %param.22, f32[32,6144]{1,0:T(8,128)S(1)} %sub.23), kind=kOutput, calls=%fused_computation.55 | convolution fusion | flops 603979776 | bytes 7110656 | tf_op jit(solution)/shard_map/jkr,lr->jkl/dot_general | solution.py:110
  327.4 41.1 %psum.29 = f32[8,32,32]{1,2,0:T(8,128)S(1)} all-reduce(f32[8,32,32]{1,2,0:T(8,128)S(1)} %convolution_bitcast_fusion.2), channel_id=1, replica_groups=mesh['sec'=2,'grp'=4,'dev'=4] {'sec','grp','dev'}, use_global_device_ids=true, to_apply=%region_12.13 | all-reduce | flops 8192 | bytes 65536 | tf_op jit(solution)/shard_map/psum | solution.py:109
  368.5 7.6 %fusion.14 = f32[32,6144]{1,0:T(8,128)S(1)} fusion(f32[32,6144]{1,0:T(8,128)S(1)} %sub.23, f32[8,32,32]{1,2,0:T(8,128)S(1)} %psum.29, f32[8,32,6144]{2,1,0:T(8,128)} %param.22), kind=kOutput, calls=%fused_computation.49 | convolution fusion | flops 604176384 | bytes 7897088 | tf_op jit(solution)/shard_map/jkl,jkr->lr/dot_general | solution.py:112
  376.8 75.2 %psum.30 = f32[32,32]{0,1:T(8,128)S(1)} all-reduce(f32[32,32]{0,1:T(8,128)S(1)} %fusion.38), channel_id=1, replica_groups=mesh['sec'=2,'grp'=4,'dev'=4] {'grp','dev'}, use_global_device_ids=true, to_apply=%region_13.14 | all-reduce | flops 1024 | bytes 8192 | tf_op jit(solution)/shard_map/psum | solution.py:114
  452.1 3.3 psum.31
  455.5 2.9 cholesky.16
  459.8 2.4 custom-call.6
  462.2 1.7 fusion.30
  (51 shorter events, 12.4 us)
Async XLA Ops:
  23.1 36.9 %all-to-all-start = ((f32[32,1,392]{2,1,0:T(1,128)}), f32[32,1,392]{2,1,0:T(1,128)S(1)}, u32[]{:S(2)}, u32[]{:S(2)}) async-start(f32[32,1,392]{2,1,0:T(1,128)} %all_to_all.9), calls=%async_computation | async-start | bytes 131072 | tf_op jit(solution)/shard_map/all_to_all | solution.py:80
  60.0 5.9 %copy-start = (f32[32,6144]{1,0:T(8,128)S(1)}, f32[32,6144]{1,0:T(8,128)}, u32[]{:S(2)}) copy-start(f32[32,6144]{1,0:T(8,128)} %param.21) | copy-start | bytes 2359300
  60.0 67.0 %copy-start.3 = (f32[1,4,1536]{2,1,0:T(4,128)S(1)}, f32[1,4,1536]{2,1,0:T(4,128)}, u32[]{:S(2)}) copy-start(f32[1,4,1536]{2,1,0:T(4,128)} %param.26) | copy-start | bytes 73732
  60.0 67.0 %copy-start.4 = (s32[1,4,1536]{2,1,0:T(4,128)S(1)}, s32[1,4,1536]{2,1,0:T(4,128)}, u32[]{:S(2)}) copy-start(s32[1,4,1536]{2,1,0:T(4,128)} %param.25) | copy-start | bytes 73732
  60.0 67.1 %copy-start.5 = (f32[6144]{0:T(1024)S(1)}, f32[6144]{0:T(1024)}, u32[]{:S(2)}) copy-start(f32[6144]{0:T(1024)} %param.27) | copy-start | bytes 73732
  60.0 67.1 %copy-start.6 = (s32[64,6]{0,1:T(8,128)S(1)}, s32[64,6]{0,1:T(8,128)}, u32[]{:S(2)}) copy-start(s32[64,6]{0,1:T(8,128)} %param.24) | copy-start | bytes 4612
  60.0 67.0 %all-to-all-start.1 = ((f32[32,32,392]{2,1,0:T(8,128)}), f32[32,32,392]{2,1,0:T(8,128)S(1)}, u32[]{:S(2)}, u32[]{:S(2)}) async-start(f32[32,32,392]{2,1,0:T(8,128)} %copy.125), calls=%async_computation.1 | async-start | bytes 4194304 | tf_op jit(solution)/shard_map/all_to_all | solution.py:79
  66.7 60.3 %collective-permute-start.2 = (f32[32,1536]{1,0:T(8,128)}, f32[32,1536]{1,0:T(8,128)}, u32[]{:S(2)}, u32[]{:S(2)}) collective-permute-start(f32[32,1536]{1,0:T(8,128)} %get-tuple-element.226), channel_id=1, source_target_pairs={{0,1},{1,0},{2,3},{3,2},{4,5},{5,4},{6,7},{7,6},{8,9},{9,8},{10,11... | collective-permute-start | bytes 589832 | tf_op jit(solution)/shard_map/ppermute | solution.py:18
  68.4 58.6 %collective-permute-start.3 = (f32[32,1536]{1,0:T(8,128)}, f32[32,1536]{1,0:T(8,128)}, u32[]{:S(2)}, u32[]{:S(2)}) collective-permute-start(f32[32,1536]{1,0:T(8,128)} %get-tuple-element.225), channel_id=1, source_target_pairs={{0,2},{2,0},{1,3},{3,1},{4,6},{6,4},{5,7},{7,5},{8,10},{10,8},{9,1... | collective-permute-start | bytes 589832 | tf_op jit(solution)/shard_map/ppermute | solution.py:18
  70.8 56.1 %collective-permute-start.4 = (f32[32,1536]{1,0:T(8,128)S(1)}, f32[32,1536]{1,0:T(8,128)}, u32[]{:S(2)}, u32[]{:S(2)}) collective-permute-start(f32[32,1536]{1,0:T(8,128)S(1)} %get-tuple-element.224), channel_id=1, source_target_pairs={{0,4},{4,0},{8,12},{12,8},{1,5},{5,1},{9,13},{13,9},{2,6},{6,2},{1... | collective-permute-start | bytes 589832 | tf_op jit(solution)/shard_map/ppermute | solution.py:18
  72.3 54.7 %collective-permute-start.5 = (f32[32,1536]{1,0:T(8,128)S(1)}, f32[32,1536]{1,0:T(8,128)}, u32[]{:S(2)}, u32[]{:S(2)}) collective-permute-start(f32[32,1536]{1,0:T(8,128)S(1)} %get-tuple-element.223), channel_id=1, source_target_pairs={{0,8},{8,0},{4,12},{12,4},{1,9},{9,1},{5,13},{13,5},{2,10},{10,2},... | collective-permute-start | bytes 589832 | tf_op jit(solution)/shard_map/ppermute | solution.py:18
  73.9 35.4 %collective-permute-start = (f32[32,1]{1,0:T(8,128)S(1)}, f32[32,1]{1,0:T(8,128)S(1)}, u32[]{:S(2)}, u32[]{:S(2)}) collective-permute-start(f32[32,1]{1,0:T(8,128)S(1)} %get-tuple-element.228), channel_id=1, source_target_pairs={{0,1},{1,2},{2,3},{3,4},{4,5},{5,6},{6,7},{7,8},{8,9},{9,10},{10,1... | collective-permute-start | bytes 392 | tf_op jit(solution)/shard_map/ppermute | solution.py:28
  109.3 16.5 %collective-permute-start.1 = (f32[32,1]{1,0:T(8,128)S(1)}, f32[32,1]{1,0:T(8,128)S(1)}, u32[]{:S(2)}, u32[]{:S(2)}) collective-permute-start(f32[32,1]{1,0:T(8,128)S(1)} %get-tuple-element.227), channel_id=1, source_target_pairs={{1,0},{2,1},{3,2},{4,3},{5,4},{6,5},{7,6},{8,7},{9,8},{10,9},{11,1... | collective-permute-start | bytes 392 | tf_op jit(solution)/shard_map/ppermute | solution.py:29
